TPU v7x, 128 devices: a whole 4x4x4 slice. The times are simulated.
128 devices in a mesh: req: 8 (over y, core), row: 4 (over z), col: 4 (over x).
Axes of the slice: x: 4, y: 4, z: 4, core: 2. Of those that a mesh axis runs over, the one named last changes fastest.
Arguments:
- tokens: bfloat16 [16384, 1024], P(('req', 'row')), may hold values from -6 to 6
- norm_gain: float32 [1024], replicated, may hold values from 0.5 to 1.5
- w_attn: bfloat16 [5, 1024, 1024], P(None, 'row', 'col'), may hold values from -1 to 1
- persist_kv: bfloat16 [2, 16, 1024], P(None, None, 'col'), may hold values from -6 to 6
- kv_pool: bfloat16 [32, 32, 1, 256, 2, 1024], P(('req', 'row'), None, None, None, None, 'col'), may hold values from -6 to 6
- cache_len: int32 [32], replicated, may hold values from 0 to 8192, as said below
- mem_state: float32 [32, 8, 128, 128], P(('req', 'row'), 'col'), may hold values from -0.5 to 0.5
- decay: float32 [32, 8, 8], P(('req', 'row'), None, 'col'), may hold values from 0.6 to 1
- rate: float32 [32, 8, 8], P(('req', 'row'), None, 'col'), may hold values from 0.05 to 0.5
Outputs:
- mixed: bfloat16 [16384, 1024], P(('req', 'row'), 'col')
- new_state: float32 [32, 8, 128, 128], P(('req', 'row'), 'col')
Inputs may be any that keep to these rules, and one draw needn't show every extreme that they name: `cache_len`: cached tokens before each block; some block has exactly 8192.
All inputs are finite; a program needn't handle non-finite values.
Results may differ from a plain program's by a relative error of at most 0.006.
Values may be sent and summed in bfloat16 or wider, within the bound.
A program may use at most 192 MiB of HBM per device.

v0:
```python
import jax
import jax.numpy as jnp
from jax import lax
from jax.sharding import PartitionSpec as P

HD = 128
NP = 16
SEG = 64
negative_fill = -1e30


def attend(query_heads, key_heads, value_heads, allowed):
    scores = jnp.einsum(
        "...shd,...khd->...hsk", query_heads, key_heads, preferred_element_type=jnp.float32
    ) * query_heads.shape[-1] ** (-0.5)
    allowed = allowed[..., None, :, :]
    scores = jnp.where(allowed, scores, negative_fill)
    maxima = jnp.max(scores, axis=-1)
    probabilities = jnp.where(allowed, jnp.exp(scores - maxima[..., None]), 0.0)
    totals = jnp.sum(probabilities, axis=-1)
    weighted = jnp.einsum(
        "...hsk,...khd->...shd",
        probabilities.astype(jnp.bfloat16),
        value_heads,
        preferred_element_type=jnp.float32,
    )
    return (weighted, jnp.swapaxes(maxima, -1, -2), jnp.swapaxes(totals, -1, -2))


def combine_parts(first_part, second_part):
    output_a, maxima_a, totals_a = first_part
    output_b, maxima_b, totals_b = second_part
    highest = jnp.maximum(maxima_a, maxima_b)
    factor_a = jnp.exp(maxima_a - highest)
    factor_b = jnp.exp(maxima_b - highest)
    merged = output_a * factor_a[..., None] + output_b * factor_b[..., None]
    return (merged, highest, totals_a * factor_a + totals_b * factor_b)


def shards(tokens, norm_gain, w_attn, persist_kv, kv_pool, cache_len, mem_state, decay, rate):
    pool_size = lax.axis_size(("req", "row"))
    my_index = lax.axis_index(("req", "row"))
    column = lax.axis_index("col")
    length = tokens.shape[0]
    local_width = w_attn.shape[2]
    heads_here = local_width // HD
    xfloat = tokens.astype(jnp.float32)
    normed = (
        xfloat * lax.rsqrt(jnp.mean(xfloat * xfloat, axis=-1, keepdims=True) + 1e-05) * norm_gain
    ).astype(jnp.bfloat16)
    gathered = lax.all_gather(w_attn, "row", axis=1, tiled=True)
    projected = jnp.einsum("sd,wdc->wsc", normed, gathered[:4], preferred_element_type=jnp.float32)
    queries = projected[0].astype(jnp.bfloat16).reshape(length, heads_here, HD)
    keys_own = projected[1].astype(jnp.bfloat16).reshape(length, heads_here, HD)
    values_own = projected[2].astype(jnp.bfloat16).reshape(length, heads_here, HD)
    gate_open = jax.nn.sigmoid(projected[3]).reshape(length, heads_here, HD)
    persist = persist_kv.reshape(2, NP, heads_here, HD)
    keys_cat = jnp.concatenate([persist[0], keys_own], axis=0)
    vals_cat = jnp.concatenate([persist[1], values_own], axis=0)
    positions = jnp.arange(length, dtype=jnp.int32)
    causal = positions[:, None] >= positions[None, :]
    allowed = jnp.concatenate([jnp.ones((length, NP), dtype=bool), causal], axis=1)
    local_part = attend(queries, keys_cat, vals_cat, allowed)
    page_pool = kv_pool[0]
    slot_count = page_pool.shape[1]
    page_len = page_pool.shape[2]
    slot_ids = jnp.arange(slot_count, dtype=jnp.int32)[None, :, None]
    offsets = jnp.arange(page_len, dtype=jnp.int32)[None, None, :]
    peer_ids = jnp.arange(pool_size, dtype=jnp.int32)[:, None, None]
    everyone = lax.all_gather(queries[None], ("req", "row"), axis=0, tiled=True)
    page_ids = slot_ids * pool_size + (my_index - peer_ids) % pool_size
    places = (page_ids * page_len + offsets).reshape(pool_size, slot_count * page_len)
    usable = (places < cache_len[:, None])[:, None, :]
    cache_keys = page_pool[:, :, :, 0].reshape(pool_size, slot_count * page_len, heads_here, HD)
    cache_vals = page_pool[:, :, :, 1].reshape(pool_size, slot_count * page_len, heads_here, HD)
    part_out, part_max, part_tot = attend(everyone, cache_keys, cache_vals, usable)
    got_out, got_max, got_tot = (
        lax.all_to_all(part_out, ("req", "row"), split_axis=0, concat_axis=0, tiled=True),
        lax.all_to_all(part_max, ("req", "row"), split_axis=0, concat_axis=0, tiled=True),
        lax.all_to_all(part_tot, ("req", "row"), split_axis=0, concat_axis=0, tiled=True),
    )
    highest = jnp.max(got_max, axis=0)
    scaling = jnp.exp(got_max - highest[None])
    cache_part = (
        jnp.sum(got_out * scaling[..., None], axis=0),
        highest,
        jnp.sum(got_tot * scaling, axis=0),
    )
    total_part = combine_parts(local_part, cache_part)
    attended = total_part[0] / total_part[2][..., None]
    query_float = queries.astype(jnp.float32)
    key_float = keys_own.astype(jnp.float32)
    value_float = values_own.astype(jnp.float32)
    query_unit = query_float * lax.rsqrt(
        jnp.sum(query_float * query_float, axis=-1, keepdims=True) + 1e-06
    )
    key_unit = key_float * lax.rsqrt(jnp.sum(key_float * key_float, axis=-1, keepdims=True) + 1e-06)
    memory = mem_state[0]
    outputs = []
    for segment in range(length // SEG):
        lower = segment * SEG
        seg_query = query_unit[lower : lower + SEG]
        seg_keys = key_unit[lower : lower + SEG]
        seg_values = value_float[lower : lower + SEG]
        outputs.append(
            jnp.einsum("shd,hde->she", seg_query, memory, precision=lax.Precision.HIGHEST)
        )
        errors = (
            jnp.einsum("shd,hde->she", seg_keys, memory, precision=lax.Precision.HIGHEST)
            - seg_values
        )
        update = jnp.einsum("shd,she->hde", seg_keys, errors, precision=lax.Precision.HIGHEST)
        memory = (
            decay[0, segment][:, None, None] * memory - rate[0, segment][:, None, None] * update
        )
    recalled = jnp.concatenate(outputs, axis=0)
    combined = (attended + gate_open * recalled).reshape(length, local_width).astype(jnp.bfloat16)
    output_terms = lax.dot_general(
        combined, gathered[4], (((1,), (1,)), ((), ())), preferred_element_type=jnp.float32
    )
    summed = lax.psum_scatter(
        output_terms.astype(jnp.bfloat16), "col", scatter_dimension=1, tiled=True
    ).astype(jnp.float32)
    own_cols = lax.dynamic_slice_in_dim(xfloat, column * summed.shape[1], summed.shape[1], 1)
    mixed = (own_cols + summed).astype(jnp.bfloat16)
    return (mixed, memory[None])


def solution(mesh):
    return jax.shard_map(
        shards,
        mesh=mesh,
        in_specs=(
            P(("req", "row"), None),
            P(),
            P(None, "row", "col"),
            P(None, None, "col"),
            P(("req", "row"), None, None, None, None, "col"),
            P(),
            P(("req", "row"), "col", None, None),
            P(("req", "row"), None, "col"),
            P(("req", "row"), None, "col"),
        ),
        out_specs=(P(("req", "row"), "col"), P(("req", "row"), "col", None, None)),
        check_vma=False,
    )
```

profile of v0, /device:TPU:0, one launch (start us, length us, event | category | flops | bytes accessed | tf_op | source)
XLA Modules:
  0.0 469.1 jit_solution(4142681741803543050)
XLA Ops:
  7.2 2.2 copy.50
  9.4 1.5 multiply_reduce_fusion.1
  11.0 39.7 %all-gather.3.cloned.1.call-done = bf16[5,1024,256]{1,2,0:T(8,128)(2,1)} async-done(((bf16[5,256,256]{1,2,0:T(8,128)(2,1)}), bf16[5,1024,256]{1,2,0:T(8,128)(2,1)}) %all-gather.3.cloned.1.call-update) | async-done | bytes 2621456 | tf_op jit(solution)/shard_map/all_gather | solution.py:51
  50.7 3.3 fusion.109
  54.0 1.4 copy-done.9
  56.3 20.9 %copy.57 = bf16[1,32,1,256,2,256]{3,5,1,4,2,0:T(8,128)(2,1)} copy(bf16[1,32,1,256,2,256]{5,4,3,2,1,0:T(2,128)(2,1)} %param.13) | data formatting | bytes 16777216 | tf_op args[4]
  77.3 6.0 %fusion.106 = (bf16[32,1,256,1,256]{2,4,0,3,1:T(8,128)(2,1)}, bf16[32,1,256,1,256]{2,4,0,3,1:T(8,128)(2,1)}) fusion(bf16[32,1,256,2,256]{2,4,0,3,1:T(8,128)(2,1)} %bitcast.129), kind=kLoop, calls=%fused_computation.168 | loop fusion | bytes 16777216 | tf_op jit(solution)/shard_map/slice | solution.py:74
  83.3 26.7 %all-gather.5.cloned.1.call-done = bf16[32,512,2,128]{3,1,2,0:T(8,128)(2,1)} async-done(((bf16[1,512,2,128]{3,1,2,0:T(8,128)(2,1)}), bf16[32,512,2,128]{3,1,2,0:T(8,128)(2,1)}) %all-gather.5.cloned.1.call-update) | async-done | bytes 8388624 | tf_op jit(solution)/shard_map/all_gather | solution.py:70
  110.1 18.0 %fusion = (f32[32,2,512]{2,1,0:T(2,128)}, f32[32,2,512,256]{2,3,1,0:T(8,128)}) fusion(pred[32,256]{1,0:T(8,128)(4,1)S(1)} %add_compare_fusion, bf16[32,512,2,128]{3,1,2,0:T(8,128)(2,1)} %all-gather.5.cloned.1.call-done, bf16[32,256,2,128]{1,3,2,0:T(8,128)(2,1)} %bitcast.130), kind=kOutput, calls=%fused_computation.2 | convolution fusion | flops 2172616704 | bytes 46276608 | tf_op jit(solution)/shard_map/...shd,...khd->...hsk/dot_general | solution.py:13
  128.1 5.5 %all-to-all-start = ((f32[32,512,2]{1,2,0:T(2,128)}), f32[32,512,2]{1,2,0:T(2,128)S(1)}, u32[]{:S(2)}, u32[]{:S(2)}) async-start(f32[32,512,2]{1,2,0:T(2,128)} %bitcast.10), calls=%async_computation | async-start | bytes 262144 | tf_op jit(solution)/shard_map/all_to_all | solution.py:79
  133.6 16.1 %fusion.1 = f32[32,2,512]{2,1,0:T(2,128)} fusion(f32[32,2,512,256]{2,3,1,0:T(8,128)} %get-tuple-element.34, f32[32,2,512]{2,1,0:T(2,128)} %get-tuple-element.33, pred[32,256]{1,0:T(8,128)(4,1)S(1)} %add_compare_fusion), kind=kLoop, calls=%fused_computation.3 | loop fusion | flops 41910272 | bytes 33824768 | tf_op jit(solution)/shard_map/reduce_sum | solution.py:20
  149.6 7.6 %all-to-all-start.2 = ((f32[32,512,2]{1,2,0:T(2,128)}), f32[32,512,2]{1,2,0:T(2,128)S(1)}, u32[]{:S(2)}, u32[]{:S(2)}) async-start(f32[32,512,2]{1,2,0:T(2,128)} %bitcast.14), calls=%async_computation.2 | async-start | bytes 262144 | tf_op jit(solution)/shard_map/all_to_all | solution.py:80
  157.2 22.5 %fusion.10 = f32[32,512,2,128]{3,1,2,0:T(8,128)} fusion(bf16[32,256,2,128]{1,3,2,0:T(8,128)(2,1)} %bitcast.131, f32[32,2,512,256]{2,3,1,0:T(8,128)} %get-tuple-element.34, f32[32,2,512]{2,1,0:T(2,128)} %get-tuple-element.33, pred[32,256]{1,0:T(8,128)(4,1)S(1)} %add_compare_fusion), kind=kOutput, calls=%fused_computation.12 | convolution fusion | flops 2189426688 | bytes 54665216 | tf_op jit(solution)/shard_map/...hsk,...khd->...shd/dot_general | solution.py:21
  180.4 7.3 %all-to-all-start.1 = ((f32[32,512,2,128]{3,1,2,0:T(8,128)}), f32[32,512,2,128]{3,1,2,0:T(8,128)}, u32[]{:S(2)}, u32[]{:S(2)}) async-start(f32[32,512,2,128]{3,1,2,0:T(8,128)} %fusion.10), calls=%async_computation.1 | async-start | bytes 33554432 | tf_op jit(solution)/shard_map/all_to_all | solution.py:78
  194.2 1.2 fusion.27
  197.9 1.2 fusion.28
  215.9 2.0 fusion.57
  219.2 190.2 %all-to-all-done.1 = f32[32,512,2,128]{3,1,2,0:T(8,128)} async-done(((f32[32,512,2,128]{3,1,2,0:T(8,128)}), f32[32,512,2,128]{3,1,2,0:T(8,128)}, u32[]{:S(2)}, u32[]{:S(2)}) %all-to-all-start.1) | async-done | bytes 16777248 | tf_op jit(solution)/shard_map/all_to_all | solution.py:78
  409.4 7.6 %multiply_reduce_fusion = f32[512,2,128]{2,0,1:T(8,128)S(1)} fusion(f32[32,512,2,128]{3,1,2,0:T(8,128)} %all-to-all-done.1, f32[32,512,2]{1,2,0:T(2,128)S(1)} %get-tuple-element.22), kind=kLoop, calls=%fused_computation.6 | loop fusion | flops 8257536 | bytes 17432576 | tf_op jit(solution)/shard_map/reduce_sum | solution.py:85
  418.1 2.5 fusion.25
  420.6 2.5 convolution_convert_fusion
  424.5 1.9 fusion.34
  426.4 34.4 %reduce-scatter.2.cloned.1.call-done = bf16[512,256]{1,0:T(8,128)(2,1)} async-done(((bf16[512,1024]{1,0:T(8,128)(2,1)}), bf16[512,256]{1,0:T(8,128)(2,1)}) %reduce-scatter.2.cloned.1.call-update) | async-done | bytes 262160 | tf_op jit(solution)/shard_map/reduce_scatter | solution.py:121
  460.9 1.7 add_convert_fusion
  (88 shorter events, 30.8 us)
Async XLA Ops:
  7.2 43.5 %all-gather.3.cloned.1.call-start = ((), (), s32[]{:S(2)}) async-start(), calls=%async_computation.4 | async-start | bytes 3276800 | tf_op jit(solution)/shard_map/all_gather | solution.py:51
  9.4 100.7 %all-gather.5.cloned.1.call-start = ((), (), s32[]{:S(2)}) async-start(), calls=%async_computation.5 | async-start | bytes 8650752 | tf_op jit(solution)/shard_map/all_gather | solution.py:70
  54.0 1.4 copy-start.9
  56.3 21.0 %copy-start.13 = (s32[32]{0:T(128)S(1)}, s32[32]{0:T(128)}, u32[]{:S(2)}) copy-start(s32[32]{0:T(128)} %param.14) | copy-start | bytes 388
  128.1 21.6 %all-to-all-start = ((f32[32,512,2]{1,2,0:T(2,128)}), f32[32,512,2]{1,2,0:T(2,128)S(1)}, u32[]{:S(2)}, u32[]{:S(2)}) async-start(f32[32,512,2]{1,2,0:T(2,128)} %bitcast.10), calls=%async_computation | async-start | bytes 262144 | tf_op jit(solution)/shard_map/all_to_all | solution.py:79
  149.6 30.1 %all-to-all-start.2 = ((f32[32,512,2]{1,2,0:T(2,128)}), f32[32,512,2]{1,2,0:T(2,128)S(1)}, u32[]{:S(2)}, u32[]{:S(2)}) async-start(f32[32,512,2]{1,2,0:T(2,128)} %bitcast.14), calls=%async_computation.2 | async-start | bytes 262144 | tf_op jit(solution)/shard_map/all_to_all | solution.py:80
  179.7 8.1 %copy-start.12 = (bf16[2,16,256]{2,1,0:T(8,128)(2,1)S(1)}, bf16[2,16,256]{2,1,0:T(8,128)(2,1)}, u32[]{:S(2)}) copy-start(bf16[2,16,256]{2,1,0:T(8,128)(2,1)} %param.12) | copy-start | bytes 49156
  179.7 9.0 %copy-start.10 = (f32[1,8,2]{1,2,0:T(2,128)S(1)}, f32[1,8,2]{1,2,0:T(2,128)}, u32[]{:S(2)}) copy-start(f32[1,8,2]{1,2,0:T(2,128)} %param.17) | copy-start | bytes 196
  179.7 9.0 %copy-start.11 = (f32[1,8,2]{1,2,0:T(2,128)S(1)}, f32[1,8,2]{1,2,0:T(2,128)}, u32[]{:S(2)}) copy-start(f32[1,8,2]{1,2,0:T(2,128)} %param.16) | copy-start | bytes 196
  179.7 0.7 copy-start.7
  180.4 229.0 %all-to-all-start.1 = ((f32[32,512,2,128]{3,1,2,0:T(8,128)}), f32[32,512,2,128]{3,1,2,0:T(8,128)}, u32[]{:S(2)}, u32[]{:S(2)}) async-start(f32[32,512,2,128]{3,1,2,0:T(8,128)} %fusion.10), calls=%async_computation.1 | async-start | bytes 33554432 | tf_op jit(solution)/shard_map/all_to_all | solution.py:78
  187.7 2.7 copy-start.4
  187.7 273.1 %reduce-scatter.2.cloned.1.call-start = ((), (), s32[]{:S(2)}) async-start(), calls=%async_computation.6 | async-start | bytes 1310720 | tf_op jit(solution)/shard_map/reduce_scatter | solution.py:121
  189.3 1.1 copy-start.6
  189.8 2.0 copy-start.2
  190.5 2.5 copy-start.3
  191.1 0.8 copy-start
  195.5 22.4 %copy-start.5 = (pred[512,528]{0,1:T(8,128)(4,1)S(1)}, pred[512,528]{0,1:T(8,128)(4,1)}, u32[]{:S(2)}) copy-start(pred[512,528]{0,1:T(8,128)(4,1)} %concatenate.13) | copy-start | bytes 811012
  214.8 4.2 copy-start.8
  418.1 5.0 %copy-start.1 = (bf16[512,1024]{1,0:T(8,128)(2,1)S(1)}, bf16[512,1024]{1,0:T(8,128)(2,1)}, u32[]{:S(2)}) copy-start(bf16[512,1024]{1,0:T(8,128)(2,1)} %param.9) | copy-start | bytes 3145732
Sparse Core Ops, SparseCore 0:
  9.6 40.9 all-gather.2
  56.4 53.6 all-gather.4
  423.3 37.5 reduce-scatter.1
where the time goes:
time: 471 us; the launch traced here: 469 us
  waiting for transfers between devices  291 us (62%)
  matrix products  76.2 us (16%)
  local copies, waits for them, and re-layouts  36 us (8%)
  other arithmetic  31 us (7%)
  starting transfers between devices  20.5 us (4%)
  between operations  14.2 us (3%)
    all_to_all x1, waiting for transfers between devices, shards(): lax.all_to_all(part_out, ('req', 'row'), split_axis=0, concat_axis=0, til...  190 us
    all_gather x1, waiting for transfers between devices, shards(): gathered = lax.all_gather(w_attn, 'row', axis=1, tiled=True)  39.7 us
    reduce_scatter x1, waiting for transfers between devices, shards(): lax.psum_scatter(output_terms.astype(jnp.bfloat16), 'col', scatter_dimens...  34.4 us
    all_gather x1, waiting for transfers between devices, shards(): everyone = lax.all_gather(queries[None], ('req', 'row'), axis=0, tiled=True)  26.7 us
    unnamed x30, local copies, waits for them, and re-layouts  25.3 us
    dot_general x2, matrix products, attend(): jnp.einsum('...hsk,...khd->...shd', probabilities.astype(jnp.bfloat16), v...  25 us
    dot_general x2, matrix products, attend(): jnp.einsum('...shd,...khd->...hsk', query_heads, key_heads, preferred_ele...  18.5 us
    reduce_sum x2, other arithmetic, attend(): totals = jnp.sum(probabilities, axis=-1)  16.6 us
  transfers between devices with their start and end apart: 6, of which 4 were waited for; matrix products, arithmetic and copies ran while one was open for 22% of the time, Pallas kernels for 0%

commit v1 on v0

--- a/solution.py
+++ b/solution.py
@@ -48,7 +48,24 @@
     normed = (
         xfloat * lax.rsqrt(jnp.mean(xfloat * xfloat, axis=-1, keepdims=True) + 1e-05) * norm_gain
     ).astype(jnp.bfloat16)
-    gathered = lax.all_gather(w_attn, "row", axis=1, tiled=True)
+    size, index, extent = (lax.axis_size("row"), lax.axis_index("row"), w_attn.shape[1])
+    right = [(i, (i + 1) % size) for i in range(size)]
+    behind = [(i, (i - 1) % size) for i in range(size)]
+    out = jnp.zeros((*w_attn.shape[:1], size * extent, *w_attn.shape[1 + 1 :]), w_attn.dtype)
+    out = lax.dynamic_update_slice_in_dim(out, w_attn, index * extent, axis=1)
+    from_left = from_right = w_attn
+    half = size // 2
+    for step in range(1, half + 1):
+        from_left = lax.ppermute(from_left, "row", right)
+        out = lax.dynamic_update_slice_in_dim(
+            out, from_left, (index - step) % size * extent, axis=1
+        )
+        if step < size - half:
+            from_right = lax.ppermute(from_right, "row", behind)
+            out = lax.dynamic_update_slice_in_dim(
+                out, from_right, (index + step) % size * extent, axis=1
+            )
+    gathered = out
     projected = jnp.einsum("sd,wdc->wsc", normed, gathered[:4], preferred_element_type=jnp.float32)
     queries = projected[0].astype(jnp.bfloat16).reshape(length, heads_here, HD)
     keys_own = projected[1].astype(jnp.bfloat16).reshape(length, heads_here, HD)

time: 471 us -> 462 us (0.981)
  waiting for transfers between devices: 291 us -> 271 us
    all_gather x1 -> x0, waiting for transfers between devices: 39.7 us -> none  [shards(): gathered = lax.all_gather(w_attn, 'row', axis=1, tiled=True)]
    ppermute x0 -> x3, waiting for transfers between devices: none -> 30.8 us  [the longest x2 30.8 us: shards(): from_left = lax.ppermute(from_left, 'row', right)]
    all_to_all x1, waiting for transfers between devices: 190 us -> 182 us  [shards(): lax.all_to_all(part_out, ('req', 'row'), split_axis=0, concat_axis=0, til...]
    unnamed x30 -> x52, local copies, waits for them, and re-layouts: 25.3 us -> 25.1 us
  transfers between devices with their start and end apart: 6 -> 8, of which waited for: 4 -> 5; matrix products, arithmetic and copies ran while one was open for 22% -> 24% of each run, Pallas kernels for 0% -> 0%
where the time goes in v1:
time: 462 us; the launch traced here: 460 us
  waiting for transfers between devices  271 us (59%)
  matrix products  80 us (17%)
  local copies, waits for them, and re-layouts  38.1 us (8%)
  other arithmetic  31.5 us (7%)
  starting transfers between devices  24.9 us (5%)
  between operations  14.7 us (3%)
    all_to_all x1, waiting for transfers between devices, shards(): lax.all_to_all(part_out, ('req', 'row'), split_axis=0, concat_axis=0, til...  182 us
    reduce_scatter x1, waiting for transfers between devices, shards(): lax.psum_scatter(output_terms.astype(jnp.bfloat16), 'col', scatter_dimens...  33 us
    ppermute x2, waiting for transfers between devices, shards(): from_left = lax.ppermute(from_left, 'row', right)  30.8 us
    unnamed x52, local copies, waits for them, and re-layouts  25.1 us
    dot_general x2, matrix products, attend(): jnp.einsum('...hsk,...khd->...shd', probabilities.astype(jnp.bfloat16), v...  25.1 us
    all_gather x1, waiting for transfers between devices, shards(): everyone = lax.all_gather(queries[None], ('req', 'row'), axis=0, tiled=True)  24.9 us
    dot_general x2, matrix products, attend(): jnp.einsum('...shd,...khd->...hsk', query_heads, key_heads, preferred_ele...  19.2 us
    reduce_sum x2, other arithmetic, attend(): totals = jnp.sum(probabilities, axis=-1)  16.6 us
  transfers between devices with their start and end apart: 8, of which 5 were waited for; matrix products, arithmetic and copies ran while one was open for 24% of the time, Pallas kernels for 0%

profile of v1, /device:TPU:0, one launch (start us, length us, event | category | flops | bytes accessed | tf_op | source)
XLA Modules:
  0.0 459.8 jit_solution(18041870960558107222)
XLA Ops:
  8.6 2.1 collective-permute-start
  10.7 2.2 collective-permute-start.1
  13.4 14.2 %collective-permute-done = bf16[5,256,256]{1,2,0:T(8,128)(2,1)S(1)} collective-permute-done((bf16[5,256,256]{1,2,0:T(8,128)(2,1)S(1)}, bf16[5,256,256]{1,2,0:T(8,128)(2,1)S(1)}, u32[]{:S(2)}, u32[]{:S(2)}) %collective-permute-start) | collective-permute-done | bytes 655392 | tf_op jit(solution)/shard_map/ppermute | solution.py:59
  28.1 16.6 %collective-permute-done.2 = bf16[5,256,256]{1,2,0:T(8,128)(2,1)S(1)} collective-permute-done((bf16[5,256,256]{1,2,0:T(8,128)(2,1)S(1)}, bf16[5,256,256]{1,2,0:T(8,128)(2,1)S(1)}, u32[]{:S(2)}, u32[]{:S(2)}) %collective-permute-start.2) | collective-permute-done | bytes 655392 | tf_op jit(solution)/shard_map/ppermute | solution.py:59
  44.8 2.3 fusion.104
  49.4 20.9 %copy.63 = bf16[1,32,1,256,2,256]{3,5,1,4,2,0:T(8,128)(2,1)} copy(bf16[1,32,1,256,2,256]{5,4,3,2,1,0:T(2,128)(2,1)} %param.13) | data formatting | bytes 16777216 | tf_op args[4]
  70.5 6.0 %fusion.101 = (bf16[32,1,256,1,256]{2,4,0,3,1:T(8,128)(2,1)}, bf16[32,1,256,1,256]{2,4,0,3,1:T(8,128)(2,1)}) fusion(bf16[32,1,256,2,256]{2,4,0,3,1:T(8,128)(2,1)} %bitcast.130), kind=kLoop, calls=%fused_computation.170 | loop fusion | bytes 16777216 | tf_op jit(solution)/shard_map/slice | solution.py:91
  76.4 24.9 %all-gather.2.cloned.1.call-done = bf16[32,512,2,128]{3,1,2,0:T(8,128)(2,1)} async-done(((bf16[1,512,2,128]{3,1,2,0:T(8,128)(2,1)}), bf16[32,512,2,128]{3,1,2,0:T(8,128)(2,1)}) %all-gather.2.cloned.1.call-update) | async-done | bytes 8388624 | tf_op jit(solution)/shard_map/all_gather | solution.py:87
  101.3 18.0 %fusion = (f32[32,2,512]{2,1,0:T(2,128)}, f32[32,2,512,256]{2,3,1,0:T(8,128)}) fusion(pred[32,256]{1,0:T(8,128)(4,1)S(1)} %add_compare_fusion, bf16[32,512,2,128]{3,1,2,0:T(8,128)(2,1)} %all-gather.2.cloned.1.call-done, bf16[32,256,2,128]{1,3,2,0:T(8,128)(2,1)} %bitcast.131), kind=kOutput, calls=%fused_computation.2 | convolution fusion | flops 2172616704 | bytes 46276608 | tf_op jit(solution)/shard_map/...shd,...khd->...hsk/dot_general | solution.py:13
  119.3 5.5 %all-to-all-start = ((f32[32,512,2]{1,2,0:T(2,128)}), f32[32,512,2]{1,2,0:T(2,128)S(1)}, u32[]{:S(2)}, u32[]{:S(2)}) async-start(f32[32,512,2]{1,2,0:T(2,128)} %bitcast.10), calls=%async_computation | async-start | bytes 262144 | tf_op jit(solution)/shard_map/all_to_all | solution.py:96
  124.8 16.1 %fusion.1 = f32[32,2,512]{2,1,0:T(2,128)} fusion(f32[32,2,512,256]{2,3,1,0:T(8,128)} %get-tuple-element.34, f32[32,2,512]{2,1,0:T(2,128)} %get-tuple-element.33, pred[32,256]{1,0:T(8,128)(4,1)S(1)} %add_compare_fusion), kind=kLoop, calls=%fused_computation.3 | loop fusion | flops 41910272 | bytes 33824768 | tf_op jit(solution)/shard_map/reduce_sum | solution.py:20
  140.9 7.6 %all-to-all-start.2 = ((f32[32,512,2]{1,2,0:T(2,128)}), f32[32,512,2]{1,2,0:T(2,128)S(1)}, u32[]{:S(2)}, u32[]{:S(2)}) async-start(f32[32,512,2]{1,2,0:T(2,128)} %bitcast.14), calls=%async_computation.2 | async-start | bytes 262144 | tf_op jit(solution)/shard_map/all_to_all | solution.py:97
  148.5 22.5 %fusion.10 = f32[32,512,2,128]{3,1,2,0:T(8,128)} fusion(bf16[32,256,2,128]{1,3,2,0:T(8,128)(2,1)} %bitcast.132, f32[32,2,512,256]{2,3,1,0:T(8,128)} %get-tuple-element.34, f32[32,2,512]{2,1,0:T(2,128)} %get-tuple-element.33, pred[32,256]{1,0:T(8,128)(4,1)S(1)} %add_compare_fusion), kind=kOutput, calls=%fused_computation.12 | convolution fusion | flops 2189426688 | bytes 54665216 | tf_op jit(solution)/shard_map/...hsk,...khd->...shd/dot_general | solution.py:21
  171.0 7.5 %all-to-all-start.1 = ((f32[32,512,2,128]{3,1,2,0:T(8,128)}), f32[32,512,2,128]{3,1,2,0:T(8,128)}, u32[]{:S(2)}, u32[]{:S(2)}) async-start(f32[32,512,2,128]{3,1,2,0:T(8,128)} %fusion.10), calls=%async_computation.1 | async-start | bytes 33554432 | tf_op jit(solution)/shard_map/all_to_all | solution.py:95
  198.0 1.9 convolution_bitcast_fusion.5
  202.3 1.9 convolution_bitcast_fusion.4
  206.6 1.9 convolution_bitcast_fusion.3
  213.0 2.0 fusion.52
  218.4 181.8 %all-to-all-done.1 = f32[32,512,2,128]{3,1,2,0:T(8,128)} async-done(((f32[32,512,2,128]{3,1,2,0:T(8,128)}), f32[32,512,2,128]{3,1,2,0:T(8,128)}, u32[]{:S(2)}, u32[]{:S(2)}) %all-to-all-start.1) | async-done | bytes 16777248 | tf_op jit(solution)/shard_map/all_to_all | solution.py:95
  400.2 7.8 %multiply_reduce_fusion = f32[512,2,128]{2,0,1:T(8,128)S(1)} fusion(f32[32,512,2,128]{3,1,2,0:T(8,128)} %all-to-all-done.1, f32[32,512,2]{1,2,0:T(2,128)S(1)} %get-tuple-element.22), kind=kLoop, calls=%fused_computation.6 | loop fusion | flops 8257536 | bytes 17432576 | tf_op jit(solution)/shard_map/reduce_sum | solution.py:102
  408.3 2.6 fusion.20
  410.9 2.5 convolution_convert_fusion
  416.2 1.9 fusion.29
  418.1 33.0 %reduce-scatter.2.cloned.1.call-done = bf16[512,256]{1,0:T(8,128)(2,1)} async-done(((bf16[512,1024]{1,0:T(8,128)(2,1)}), bf16[512,256]{1,0:T(8,128)(2,1)}) %reduce-scatter.2.cloned.1.call-update) | async-done | bytes 262160 | tf_op jit(solution)/shard_map/reduce_scatter | solution.py:138
  (118 shorter events, 41.4 us)
Async XLA Ops:
  7.2 20.4 %copy-start.1 = (bf16[512,1024]{1,0:T(8,128)(2,1)S(1)}, bf16[512,1024]{1,0:T(8,128)(2,1)}, u32[]{:S(2)}) copy-start(bf16[512,1024]{1,0:T(8,128)(2,1)} %param.9) | copy-start | bytes 3145732
  7.2 94.2 %all-gather.2.cloned.1.call-start = ((), (), s32[]{:S(2)}) async-start(), calls=%async_computation.4 | async-start | bytes 8650752 | tf_op jit(solution)/shard_map/all_gather | solution.py:87
  8.6 18.9 %collective-permute-start = (bf16[5,256,256]{1,2,0:T(8,128)(2,1)S(1)}, bf16[5,256,256]{1,2,0:T(8,128)(2,1)S(1)}, u32[]{:S(2)}, u32[]{:S(2)}) collective-permute-start(bf16[5,256,256]{1,2,0:T(8,128)(2,1)S(1)} %copy.54), channel_id=1, source_target_pairs={{0,4},{4,8},{8,12},{12,0},{1,5},{5,9},{9,13},{13,1},{2,6},{6,10},{... | collective-permute-start | bytes 1966088 | tf_op jit(solution)/shard_map/ppermute | solution.py:59
  10.7 17.2 %collective-permute-start.1 = (bf16[5,256,256]{1,2,0:T(8,128)(2,1)S(1)}, bf16[5,256,256]{1,2,0:T(8,128)(2,1)S(1)}, u32[]{:S(2)}, u32[]{:S(2)}) collective-permute-start(bf16[5,256,256]{1,2,0:T(8,128)(2,1)S(1)} %copy.54), channel_id=1, source_target_pairs={{0,12},{4,0},{8,4},{12,8},{1,13},{5,1},{9,5},{13,9},{2,14},{6,2},{... | collective-permute-start | bytes 1966088 | tf_op jit(solution)/shard_map/ppermute | solution.py:64
  13.3 31.4 %copy-start.24 = (f32[1024]{0:T(1024)S(1)}, f32[1024]{0:T(1024)}, u32[]{:S(2)}) copy-start(f32[1024]{0:T(1024)} %param.10) | copy-start | bytes 12292
  27.6 17.1 %collective-permute-start.2 = (bf16[5,256,256]{1,2,0:T(8,128)(2,1)S(1)}, bf16[5,256,256]{1,2,0:T(8,128)(2,1)S(1)}, u32[]{:S(2)}, u32[]{:S(2)}) collective-permute-start(bf16[5,256,256]{1,2,0:T(8,128)(2,1)S(1)} %collective-permute-done), channel_id=1, source_target_pairs={{0,4},{4,8},{8,12},{12,0},{1,5},{5,9},{9,13},{13,1},{2,6},{6,10},{... | collective-permute-start | bytes 1966088 | tf_op jit(solution)/shard_map/ppermute | solution.py:59
  49.4 21.0 %copy-start.23 = (s32[32]{0:T(128)S(1)}, s32[32]{0:T(128)}, u32[]{:S(2)}) copy-start(s32[32]{0:T(128)} %param.14) | copy-start | bytes 388
  119.3 21.6 %all-to-all-start = ((f32[32,512,2]{1,2,0:T(2,128)}), f32[32,512,2]{1,2,0:T(2,128)S(1)}, u32[]{:S(2)}, u32[]{:S(2)}) async-start(f32[32,512,2]{1,2,0:T(2,128)} %bitcast.10), calls=%async_computation | async-start | bytes 262144 | tf_op jit(solution)/shard_map/all_to_all | solution.py:96
  140.9 30.1 %all-to-all-start.2 = ((f32[32,512,2]{1,2,0:T(2,128)}), f32[32,512,2]{1,2,0:T(2,128)S(1)}, u32[]{:S(2)}, u32[]{:S(2)}) async-start(f32[32,512,2]{1,2,0:T(2,128)} %bitcast.14), calls=%async_computation.2 | async-start | bytes 262144 | tf_op jit(solution)/shard_map/all_to_all | solution.py:97
  171.0 8.9 %copy-start.9 = (f32[1,8,2]{1,2,0:T(2,128)S(1)}, f32[1,8,2]{1,2,0:T(2,128)}, u32[]{:S(2)}) copy-start(f32[1,8,2]{1,2,0:T(2,128)} %param.17) | copy-start | bytes 196
  171.0 8.9 %copy-start.10 = (f32[1,8,2]{1,2,0:T(2,128)S(1)}, f32[1,8,2]{1,2,0:T(2,128)}, u32[]{:S(2)}) copy-start(f32[1,8,2]{1,2,0:T(2,128)} %param.16) | copy-start | bytes 196
  171.0 229.2 %all-to-all-start.1 = ((f32[32,512,2,128]{3,1,2,0:T(8,128)}), f32[32,512,2,128]{3,1,2,0:T(8,128)}, u32[]{:S(2)}, u32[]{:S(2)}) async-start(f32[32,512,2,128]{3,1,2,0:T(8,128)} %fusion.10), calls=%async_computation.1 | async-start | bytes 33554432 | tf_op jit(solution)/shard_map/all_to_all | solution.py:95
  178.5 272.6 %reduce-scatter.2.cloned.1.call-start = ((), (), s32[]{:S(2)}) async-start(), calls=%async_computation.5 | async-start | bytes 1310720 | tf_op jit(solution)/shard_map/reduce_scatter | solution.py:138
  182.6 9.4 %copy-start.21 = (f32[2]{0:T(128)S(1)}, f32[2]{0:T(128)}, u32[]{:S(2)}) copy-start(f32[2]{0:T(128)} %get-tuple-element.14) | copy-start | bytes 28
  182.6 9.4 %copy-start.22 = (f32[2]{0:T(128)S(1)}, f32[2]{0:T(128)}, u32[]{:S(2)}) copy-start(f32[2]{0:T(128)} %get-tuple-element.38) | copy-start | bytes 28
  183.1 12.6 %copy-start.19 = (f32[2]{0:T(128)S(1)}, f32[2]{0:T(128)}, u32[]{:S(2)}) copy-start(f32[2]{0:T(128)} %get-tuple-element.13) | copy-start | bytes 28
  183.1 12.6 %copy-start.20 = (f32[2]{0:T(128)S(1)}, f32[2]{0:T(128)}, u32[]{:S(2)}) copy-start(f32[2]{0:T(128)} %get-tuple-element.39) | copy-start | bytes 28
  184.4 15.5 %copy-start.17 = (f32[2]{0:T(128)S(1)}, f32[2]{0:T(128)}, u32[]{:S(2)}) copy-start(f32[2]{0:T(128)} %get-tuple-element.12) | copy-start | bytes 28
  184.4 15.5 %copy-start.18 = (f32[2]{0:T(128)S(1)}, f32[2]{0:T(128)}, u32[]{:S(2)}) copy-start(f32[2]{0:T(128)} %get-tuple-element.40) | copy-start | bytes 28
  184.9 19.3 %copy-start.15 = (f32[2]{0:T(128)S(1)}, f32[2]{0:T(128)}, u32[]{:S(2)}) copy-start(f32[2]{0:T(128)} %get-tuple-element.11) | copy-start | bytes 28
  184.9 19.3 %copy-start.16 = (f32[2]{0:T(128)S(1)}, f32[2]{0:T(128)}, u32[]{:S(2)}) copy-start(f32[2]{0:T(128)} %get-tuple-element.41) | copy-start | bytes 28
  188.3 20.1 %copy-start.14 = (f32[2]{0:T(128)S(1)}, f32[2]{0:T(128)}, u32[]{:S(2)}) copy-start(f32[2]{0:T(128)} %get-tuple-element.35) | copy-start | bytes 28
  190.7 20.9 %copy-start.7 = (f32[64,2,128]{0,2,1:T(8,128)S(1)}, f32[64,2,128]{0,2,1:T(8,128)}, u32[]{:S(2)}) copy-start(f32[64,2,128]{0,2,1:T(8,128)} %convolution_bitcast_fusion.9) | copy-start | bytes 196612
  400.2 8.1 %copy-start.12 = (bf16[16,2,128]{2,0,1:T(8,128)(2,1)S(1)}, bf16[16,2,128]{2,0,1:T(8,128)(2,1)}, u32[]{:S(2)}) copy-start(bf16[16,2,128]{2,0,1:T(8,128)(2,1)} %copy.57) | copy-start | bytes 24580
  (9 other events, 27.3 us)
Sparse Core Ops, SparseCore 0:
  49.5 51.7 all-gather.1
  413.5 37.4 reduce-scatter.1
